TPU v7x, 256 devices: a whole 4x4x8 slice. The times are simulated.
256 devices in a mesh: site: 2 (over core), wide: 32 (over x, z), narrow: 4 (over y).
Axes of the slice: x: 4, y: 4, z: 8, core: 2. Of those that a mesh axis runs over, the one named last changes fastest.
Arguments:
- initial_rows: float32 [64, 4, 2048], P('site', 'narrow'), may hold values from -6 to 6
- outcomes: int32 [64, 4], replicated, may hold values 0 or 1
- tensors: float32 [4, 2, 4, 2048, 8192], P('site', None, 'narrow', None, 'wide'), may hold values from -0.25 to 0.25
Outputs:
- final_rows: float32 [64, 4, 2048], P('site', 'narrow')
- log_weight: float32 [64], P('site')
All inputs are finite; a program needn't handle non-finite values.
Results may differ from a plain program's by a relative error of at most 0.0003.
Values sent between devices are 32-bit elements; how exact they have to be, the bound alone decides.
A program may use at most 64 MiB of HBM per device.

v0:
```python
import jax
import jax.numpy as jnp
from jax import lax
from jax.sharding import PartitionSpec as P

BOND = 8192
epsilon = 1e-06
highest = lax.Precision.HIGHEST


def from_partner(value, axis, distance):
    mask = 2**distance
    pairs = [(source, source ^ mask) for source in range(lax.axis_size(axis))]
    return lax.ppermute(value, axis, pairs)


def advance(held, log_sum, site_tensor, chosen):
    front = held.shape[0]
    groups = lax.axis_size("narrow")
    share = front // groups
    summed = lax.psum_scatter(
        jnp.einsum(
            "bar,oard->bod",
            held,
            site_tensor,
            precision=highest,
            preferred_element_type=jnp.float32,
        ),
        "narrow",
        scatter_dimension=0,
        tiled=True,
    )
    local_choice = lax.dynamic_slice_in_dim(chosen, lax.axis_index("narrow") * share, share, 0)
    squares = jnp.sum(summed * summed, axis=2)
    raw_kept = jnp.where(local_choice[:, None] == 0, summed[:, 0, :], summed[:, 1, :])
    totals = lax.psum(squares, "wide")
    both_mean = (totals[:, 0] + totals[:, 1]) / (2.0 * BOND)
    scale = lax.rsqrt(both_mean + epsilon)
    full_rows = lax.all_gather(raw_kept * scale[:, None], "wide", axis=1, tiled=True)
    kept_square = jnp.where(local_choice == 0, totals[:, 0], totals[:, 1])
    local_ratio = jnp.log(kept_square / BOND + epsilon) - jnp.log(both_mean + epsilon)
    ratio_table = jnp.broadcast_to(local_ratio[:, None], (share, groups))
    split_rows = full_rows.reshape(share, groups, -1)
    moved, moved_ratio = (
        lax.all_to_all(split_rows, "narrow", split_axis=1, concat_axis=0, tiled=True),
        lax.all_to_all(ratio_table, "narrow", split_axis=1, concat_axis=0, tiled=True),
    )
    return (moved, log_sum + moved_ratio[:, 0])


def run_section(held, log_sum, tensors, chosen_block):
    for local_site in range(tensors.shape[0]):
        held, log_sum = advance(held, log_sum, tensors[local_site], chosen_block[:, local_site])
    return (held, log_sum)


def hand_over(held, log_sum):
    moved_rows, moved_sum = from_partner((held, log_sum), "site", 0)
    return (moved_rows, moved_sum)


def shards(initial_rows, outcomes, tensors):
    section = lax.axis_index("site")
    front = initial_rows.shape[0]
    local_count = tensors.shape[0]
    section_columns = lax.dynamic_slice_in_dim(outcomes, section * local_count, local_count, 1)
    held = initial_rows
    log_sum = jnp.zeros((front,), jnp.float32)
    front_order = (section, 1 - section, section)
    for turn_index in range(3):
        new_rows, new_sum = run_section(
            held,
            log_sum,
            tensors,
            lax.dynamic_slice_in_dim(section_columns, front_order[turn_index] * front, front, 0),
        )
        if turn_index == 1:
            held, log_sum = (new_rows, new_sum)
        else:
            active = section == 0 if turn_index == 0 else section == 1
            held = jnp.where(active, new_rows, held)
            log_sum = jnp.where(active, new_sum, log_sum)
        if turn_index < 2:
            held, log_sum = hand_over(held, log_sum)
    return (held, log_sum)


def solution(mesh):
    placed = (P("site", "narrow", None), P(), P("site", None, "narrow", None, "wide"))
    return jax.shard_map(
        shards,
        mesh=mesh,
        in_specs=placed,
        out_specs=(P("site", "narrow", None), P("site")),
        check_vma=False,
    )
```

profile of v0, /device:TPU:2, one launch (start us, length us, event | category | flops | bytes accessed | tf_op | source)
XLA Modules:
  0.0 993.4 jit_solution(1777501969221541964)
XLA Ops:
  7.2 5.4 fusion.2
  12.7 0.8 fusion.33
  13.6 25.4 %reduce-scatter.7.cloned.1.call-done = f32[8,2,256]{2,0,1:T(8,128)} async-done(((f32[32,2,256]{2,0,1:T(8,128)}), f32[8,2,256]{2,0,1:T(8,128)}) %reduce-scatter.7.cloned.1.call-update) | async-done | bytes 16400 | tf_op jit(solution)/shard_map/reduce_scatter | solution.py:21
  39.0 0.8 multiply_reduce_fusion.5
  39.8 63.2 %psum.42 = f32[8,2]{0,1:T(2,128)S(1)} all-reduce(f32[8,2]{0,1:T(2,128)S(1)} %multiply_reduce_fusion.5), channel_id=1, replica_groups=mesh['site'=2,'wide'=32,'narrow'=4] {'wide'}, use_global_device_ids=true, to_apply=%region_2.3 | all-reduce | flops 16 | bytes 128 | tf_op jit(solution)/shard_map/psum | solution.py:36
  103.9 58.4 %all_gather.18 = f32[8,8192]{1,0:T(8,128)S(1)} all-gather(f32[8,256]{1,0:T(8,128)S(1)} %fusion.24), channel_id=1, replica_groups=mesh['site'=2,'wide'=32,'narrow'=4] {'wide'}, dimensions={1}, use_global_device_ids=true | all-gather | bytes 270336 | tf_op jit(solution)/shard_map/all_gather | solution.py:39
  162.3 9.2 all_to_all.171
  171.5 5.3 fusion.5
  176.9 18.2 %reduce-scatter.9.cloned.1.call-done = f32[8,2,256]{2,0,1:T(8,128)} async-done(((f32[32,2,256]{2,0,1:T(8,128)}), f32[8,2,256]{2,0,1:T(8,128)}) %reduce-scatter.9.cloned.1.call-update) | async-done | bytes 16400 | tf_op jit(solution)/shard_map/reduce_scatter | solution.py:21
  195.0 0.8 multiply_reduce_fusion.4
  195.9 63.2 %psum.43 = f32[8,2]{0,1:T(2,128)S(1)} all-reduce(f32[8,2]{0,1:T(2,128)S(1)} %multiply_reduce_fusion.4), channel_id=1, replica_groups=mesh['site'=2,'wide'=32,'narrow'=4] {'wide'}, use_global_device_ids=true, to_apply=%region_5.6 | all-reduce | flops 16 | bytes 128 | tf_op jit(solution)/shard_map/psum | solution.py:36
  260.0 62.4 %all_gather.19 = f32[8,8192]{1,0:T(8,128)} all-gather(f32[8,256]{1,0:T(8,128)S(1)} %fusion.22), channel_id=1, replica_groups=mesh['site'=2,'wide'=32,'narrow'=4] {'wide'}, dimensions={1}, use_global_device_ids=true | all-gather | bytes 270336 | tf_op jit(solution)/shard_map/all_gather | solution.py:39
  322.4 3.4 all-to-all-start.1
  325.9 6.6 all-to-all-done.1
  332.7 1.5 collective-permute-done
  334.2 5.3 fusion.1
  339.6 18.2 %reduce-scatter.11.cloned.1.call-done = f32[8,2,256]{2,0,1:T(8,128)} async-done(((f32[32,2,256]{2,0,1:T(8,128)}), f32[8,2,256]{2,0,1:T(8,128)}) %reduce-scatter.11.cloned.1.call-update) | async-done | bytes 16400 | tf_op jit(solution)/shard_map/reduce_scatter | solution.py:21
  357.8 0.8 multiply_reduce_fusion.3
  358.6 63.2 %psum.44 = f32[8,2]{0,1:T(2,128)S(1)} all-reduce(f32[8,2]{0,1:T(2,128)S(1)} %multiply_reduce_fusion.3), channel_id=1, replica_groups=mesh['site'=2,'wide'=32,'narrow'=4] {'wide'}, use_global_device_ids=true, to_apply=%region_8.9 | all-reduce | flops 16 | bytes 128 | tf_op jit(solution)/shard_map/psum | solution.py:36
  422.8 58.4 %all_gather.20 = f32[8,8192]{1,0:T(8,128)S(1)} all-gather(f32[8,256]{1,0:T(8,128)S(1)} %fusion.20), channel_id=1, replica_groups=mesh['site'=2,'wide'=32,'narrow'=4] {'wide'}, dimensions={1}, use_global_device_ids=true | all-gather | bytes 270336 | tf_op jit(solution)/shard_map/all_gather | solution.py:39
  481.1 9.2 all_to_all.172
  490.3 5.3 fusion.4
  495.7 18.1 %reduce-scatter.13.cloned.1.call-done = f32[8,2,256]{2,0,1:T(8,128)} async-done(((f32[32,2,256]{2,0,1:T(8,128)}), f32[8,2,256]{2,0,1:T(8,128)}) %reduce-scatter.13.cloned.1.call-update) | async-done | bytes 16400 | tf_op jit(solution)/shard_map/reduce_scatter | solution.py:21
  514.7 63.2 %psum.45 = f32[8,2]{0,1:T(2,128)S(1)} all-reduce(f32[8,2]{0,1:T(2,128)S(1)} %multiply_reduce_fusion.2), channel_id=1, replica_groups=mesh['site'=2,'wide'=32,'narrow'=4] {'wide'}, use_global_device_ids=true, to_apply=%region_11.12 | all-reduce | flops 16 | bytes 128 | tf_op jit(solution)/shard_map/psum | solution.py:36
  578.8 58.4 %all_gather.21 = f32[8,8192]{1,0:T(8,128)S(1)} all-gather(f32[8,256]{1,0:T(8,128)S(1)} %fusion.18), channel_id=1, replica_groups=mesh['site'=2,'wide'=32,'narrow'=4] {'wide'}, dimensions={1}, use_global_device_ids=true | all-gather | bytes 270336 | tf_op jit(solution)/shard_map/all_gather | solution.py:39
  637.2 9.2 all_to_all.173
  646.4 1.5 collective-permute-done.1
  647.9 5.3 fusion
  653.3 7.6 all_to_all.174
  661.5 3.2 all-to-all-start.7
  664.6 5.2 all-to-all-done.7
  670.0 1.4 reduce-scatter.15.cloned.1.call-done
  672.8 3.2 all-to-all-start.8
  676.0 63.3 %psum.46 = f32[8,2]{0,1:T(2,128)S(1)} all-reduce(f32[8,2]{0,1:T(2,128)S(1)} %multiply_reduce_fusion.1), channel_id=1, replica_groups=mesh['site'=2,'wide'=32,'narrow'=4] {'wide'}, use_global_device_ids=true, to_apply=%region_14.15 | all-reduce | flops 16 | bytes 128 | tf_op jit(solution)/shard_map/psum | solution.py:36
  740.7 4.7 all-to-all-start.9
  745.5 62.4 %all_gather.22 = f32[8,8192]{1,0:T(8,128)} all-gather(f32[8,256]{1,0:T(8,128)S(1)} %fusion.16), channel_id=1, replica_groups=mesh['site'=2,'wide'=32,'narrow'=4] {'wide'}, dimensions={1}, use_global_device_ids=true | all-gather | bytes 270336 | tf_op jit(solution)/shard_map/all_gather | solution.py:39
  807.9 4.8 all-to-all-start.4
  812.9 6.5 all-to-all-done.4
  819.4 5.3 fusion.3
  825.3 3.2 all-to-all-start.10
  828.6 5.1 all-to-all-done.10
  833.7 9.2 reduce-scatter.17.cloned.1.call-done
  843.8 63.2 %psum.47 = f32[8,2]{0,1:T(2,128)S(1)} all-reduce(f32[8,2]{0,1:T(2,128)S(1)} %multiply_reduce_fusion), channel_id=1, replica_groups=mesh['site'=2,'wide'=32,'narrow'=4] {'wide'}, use_global_device_ids=true, to_apply=%region_17.18 | all-reduce | flops 16 | bytes 128 | tf_op jit(solution)/shard_map/psum | solution.py:36
  907.7 3.2 all-to-all-start.11
  911.7 62.4 %all_gather.23 = f32[8,8192]{1,0:T(8,128)} all-gather(f32[8,256]{1,0:T(8,128)S(1)} %fusion.14), channel_id=1, replica_groups=mesh['site'=2,'wide'=32,'narrow'=4] {'wide'}, dimensions={1}, use_global_device_ids=true | all-gather | bytes 270336 | tf_op jit(solution)/shard_map/all_gather | solution.py:39
  974.1 4.8 all-to-all-start.5
  979.5 6.1 all-to-all-done.5
  985.6 1.0 copy.12
  (64 shorter events, 12.6 us)
Async XLA Ops:
  7.2 325.3 %copy-start = (f32[32,1,2048]{2,1,0:T(1,128)S(1)}, f32[32,1,2048]{2,1,0:T(1,128)}, u32[]{:S(2)}) copy-start(f32[32,1,2048]{2,1,0:T(1,128)} %param.3) | copy-start | bytes 786436
  7.2 31.8 %reduce-scatter.7.cloned.1.call-start = ((), (), s32[]{:S(2)}) async-start(), calls=%async_computation.18 | async-start | bytes 81920 | tf_op jit(solution)/shard_map/reduce_scatter | solution.py:21
  12.7 182.3 %reduce-scatter.9.cloned.1.call-start = ((), (), s32[]{:S(2)}) async-start(), calls=%async_computation.19 | async-start | bytes 81920 | tf_op jit(solution)/shard_map/reduce_scatter | solution.py:21
  322.4 10.1 %all-to-all-start.1 = ((f32[8,4,2048]{2,0,1:T(8,128)}), f32[8,4,2048]{2,0,1:T(8,128)S(1)}, u32[]{:S(2)}, u32[]{:S(2)}) async-start(f32[8,4,2048]{2,0,1:T(8,128)} %bitcast.19), calls=%async_computation.3 | async-start | bytes 524288 | tf_op jit(solution)/shard_map/all_to_all | solution.py:45
  325.8 31.9 %reduce-scatter.11.cloned.1.call-start = ((), (), s32[]{:S(2)}) async-start(), calls=%async_computation.20 | async-start | bytes 81920 | tf_op jit(solution)/shard_map/reduce_scatter | solution.py:21
  332.6 1.6 collective-permute-start
  339.5 174.3 %reduce-scatter.13.cloned.1.call-start = ((), (), s32[]{:S(2)}) async-start(), calls=%async_computation.21 | async-start | bytes 81920 | tf_op jit(solution)/shard_map/reduce_scatter | solution.py:21
  495.6 175.8 %reduce-scatter.15.cloned.1.call-start = ((), (), s32[]{:S(2)}) async-start(), calls=%async_computation.22 | async-start | bytes 81920 | tf_op jit(solution)/shard_map/reduce_scatter | solution.py:21
  646.4 1.5 collective-permute-start.1
  661.5 8.4 all-to-all-start.7
  670.0 154.7 %collective-permute-start.2 = (f32[32]{0:T(128)S(1)}, f32[32]{0:T(128)S(1)}, u32[]{:S(2)}, u32[]{:S(2)}) collective-permute-start(f32[32]{0:T(128)S(1)} %select_n.125), channel_id=1, source_target_pairs={{0,128},{128,0},{1,129},{129,1},{2,130},{130,2},{3,131},{131,3},{4... | collective-permute-start | bytes 392 | tf_op jit(solution)/shard_map/ppermute | solution.py:14
  672.8 67.4 %all-to-all-start.8 = ((f32[8,4,1]{0,2,1:T(1,128)}), f32[8,4,1]{0,2,1:T(1,128)S(1)}, u32[]{:S(2)}, u32[]{:S(2)}) async-start(f32[8,4,1]{0,2,1:T(1,128)} %broadcast_in_dim.99), calls=%async_computation.14 | async-start | bytes 4096 | tf_op jit(solution)/shard_map/all_to_all | solution.py:46
  740.7 67.1 %all-to-all-start.9 = ((f32[8,4,1]{0,2,1:T(1,128)}), f32[8,4,1]{0,2,1:T(1,128)S(1)}, u32[]{:S(2)}, u32[]{:S(2)}) async-start(f32[8,4,1]{0,2,1:T(1,128)} %broadcast_in_dim.100), calls=%async_computation.15 | async-start | bytes 4096 | tf_op jit(solution)/shard_map/all_to_all | solution.py:46
  807.9 11.5 %all-to-all-start.4 = ((f32[8,4,2048]{2,0,1:T(8,128)}), f32[8,4,2048]{2,0,1:T(8,128)S(1)}, u32[]{:S(2)}, u32[]{:S(2)}) async-start(f32[8,4,2048]{2,0,1:T(8,128)} %bitcast.45), calls=%async_computation.9 | async-start | bytes 524288 | tf_op jit(solution)/shard_map/all_to_all | solution.py:45
  812.7 30.3 %reduce-scatter.17.cloned.1.call-start = ((), (), s32[]{:S(2)}) async-start(), calls=%async_computation.23 | async-start | bytes 81920 | tf_op jit(solution)/shard_map/reduce_scatter | solution.py:21
  825.3 8.4 all-to-all-start.10
  828.5 150.6 %collective-permute-start.3 = (f32[32]{0:T(128)S(1)}, f32[32]{0:T(128)S(1)}, u32[]{:S(2)}, u32[]{:S(2)}) collective-permute-start(f32[32]{0:T(128)S(1)} %add_add_fusion), channel_id=1, source_target_pairs={{0,128},{128,0},{1,129},{129,1},{2,130},{130,2},{3,131},{131,3},{4... | collective-permute-start | bytes 392 | tf_op jit(solution)/shard_map/ppermute | solution.py:14
  907.7 66.4 %all-to-all-start.11 = ((f32[8,4,1]{0,2,1:T(1,128)}), f32[8,4,1]{0,2,1:T(1,128)S(1)}, u32[]{:S(2)}, u32[]{:S(2)}) async-start(f32[8,4,1]{0,2,1:T(1,128)} %broadcast_in_dim.102), calls=%async_computation.17 | async-start | bytes 4096 | tf_op jit(solution)/shard_map/all_to_all | solution.py:46
  974.1 11.4 %all-to-all-start.5 = ((f32[8,4,2048]{2,0,1:T(8,128)}), f32[8,4,2048]{2,0,1:T(8,128)S(1)}, u32[]{:S(2)}, u32[]{:S(2)}) async-start(f32[8,4,2048]{2,0,1:T(8,128)} %bitcast.53), calls=%async_computation.11 | async-start | bytes 524288 | tf_op jit(solution)/shard_map/all_to_all | solution.py:45
Sparse Core Ops, SparseCore 0:
  12.8 26.1 reduce-scatter.6
  177.0 18.0 reduce-scatter.8
  339.6 18.0 reduce-scatter.10
  495.8 18.0 reduce-scatter.12
  653.4 18.0 reduce-scatter.14
  824.8 18.0 reduce-scatter.16
where the time goes:
time: 995 us; the launch traced here: 993 us
  blocking collectives  777 us (78%)
  waiting for transfers between devices  123 us (12%)
  matrix products  31.9 us (3%)
  starting transfers between devices  30.9 us (3%)
  between operations  14.3 us (1%)
  other arithmetic  11 us (1%)
    psum x6, blocking collectives, advance(): totals = lax.psum(squares, 'wide')  379 us
    all_gather x6, blocking collectives, advance(): lax.all_gather(raw_kept * scale[:, None], 'wide', axis=1, tiled=True)  362 us
    reduce_scatter x6, waiting for transfers between devices, advance(): lax.psum_scatter(jnp.einsum('bar,oard->bod', held, site_tensor, precision...  90.4 us
    dot_general x6, matrix products, advance(): jnp.einsum('bar,oard->bod', held, site_tensor, precision=highest, preferr...  31.9 us
    all_to_all x3, blocking collectives, advance(): lax.all_to_all(split_rows, 'narrow', split_axis=1, concat_axis=0, tiled=T...  27.6 us
  transfers between devices with their start and end apart: 18, of which 13 were waited for; matrix products, arithmetic and copies ran while one was open for 1% of the time, Pallas kernels for 0%

commit v1 on v0

--- a/solution.py
+++ b/solution.py
@@ -36,7 +36,11 @@
     totals = lax.psum(squares, "wide")
     both_mean = (totals[:, 0] + totals[:, 1]) / (2.0 * BOND)
     scale = lax.rsqrt(both_mean + epsilon)
-    full_rows = lax.all_gather(raw_kept * scale[:, None], "wide", axis=1, tiled=True)
+    own = raw_kept * scale[:, None]
+    n_dev = lax.axis_size("wide")
+    blocks = jnp.stack([own for _ in range(n_dev)])
+    blocks = lax.all_to_all(blocks, "wide", split_axis=0, concat_axis=0)
+    full_rows = jnp.concatenate(blocks, axis=1)
     kept_square = jnp.where(local_choice == 0, totals[:, 0], totals[:, 1])
     local_ratio = jnp.log(kept_square / BOND + epsilon) - jnp.log(both_mean + epsilon)
     ratio_table = jnp.broadcast_to(local_ratio[:, None], (share, groups))

time: 995 us -> 804 us (0.81)
  blocking collectives: 777 us -> 532 us
  waiting for transfers between devices: 123 us -> 157 us
  starting transfers between devices: 30.9 us -> 48.1 us
    all_gather x6 -> x0, blocking collectives: 362 us -> none  [advance(): lax.all_gather(raw_kept * scale[:, None], 'wide', axis=1, tiled=True)]
    all_to_all x1 -> x5, blocking collectives: 7.62 us -> 125 us  [advance(): blocks = lax.all_to_all(blocks, 'wide', split_axis=0, concat_axis=0)]
    all_to_all x0 -> x1, starting transfers between devices: none -> 16.6 us  [advance(): blocks = lax.all_to_all(blocks, 'wide', split_axis=0, concat_axis=0)]
    reduce_scatter x6, waiting for transfers between devices: 90.4 us -> 105 us  [advance(): lax.psum_scatter(jnp.einsum('bar,oard->bod', held, site_tensor, precision...]
    all_to_all x5 -> x6, starting transfers between devices: 17.5 us -> 20.8 us  [advance(): lax.all_to_all(ratio_table, 'narrow', split_axis=1, concat_axis=0, tiled=...]
  transfers between devices with their start and end apart: 18 -> 20, of which waited for: 13 -> 16; matrix products, arithmetic and copies ran while one was open for 1% -> 1% of each run, Pallas kernels for 0% -> 0%
where the time goes in v1:
time: 804 us; the launch traced here: 801 us
  blocking collectives  532 us (66%)
  waiting for transfers between devices  157 us (20%)
  starting transfers between devices  48.1 us (6%)
  matrix products  31.9 us (4%)
  between operations  14.3 us (2%)
  other arithmetic  11 us (1%)
    psum x6, blocking collectives, advance(): totals = lax.psum(squares, 'wide')  379 us
    all_to_all x5, blocking collectives, advance(): blocks = lax.all_to_all(blocks, 'wide', split_axis=0, concat_axis=0)  125 us
    reduce_scatter x6, waiting for transfers between devices, advance(): lax.psum_scatter(jnp.einsum('bar,oard->bod', held, site_tensor, precision...  105 us
    dot_general x6, matrix products, advance(): jnp.einsum('bar,oard->bod', held, site_tensor, precision=highest, preferr...  31.9 us
    all_to_all x3, blocking collectives, advance(): lax.all_to_all(split_rows, 'narrow', split_axis=1, concat_axis=0, tiled=T...  27.6 us
    all_to_all x6, starting transfers between devices, advance(): lax.all_to_all(ratio_table, 'narrow', split_axis=1, concat_axis=0, tiled=...  20.8 us
    all_to_all x3, waiting for transfers between devices, advance(): lax.all_to_all(split_rows, 'narrow', split_axis=1, concat_axis=0, tiled=T...  19.4 us
    all_to_all x6, waiting for transfers between devices, advance(): lax.all_to_all(ratio_table, 'narrow', split_axis=1, concat_axis=0, tiled=...  19.4 us
  transfers between devices with their start and end apart: 20, of which 16 were waited for; matrix products, arithmetic and copies ran while one was open for 1% of the time, Pallas kernels for 0%

profile of v1, /device:TPU:2, one launch (start us, length us, event | category | flops | bytes accessed | tf_op | source)
XLA Modules:
  0.0 801.0 jit_solution(17320977020725761283)
XLA Ops:
  7.2 5.4 fusion.2
  12.7 0.8 fusion.33
  13.6 25.4 %reduce-scatter.7.cloned.1.call-done = f32[8,2,256]{2,0,1:T(8,128)} async-done(((f32[32,2,256]{2,0,1:T(8,128)}), f32[8,2,256]{2,0,1:T(8,128)}) %reduce-scatter.7.cloned.1.call-update) | async-done | bytes 16400 | tf_op jit(solution)/shard_map/reduce_scatter | solution.py:21
  39.8 63.2 %psum.42 = f32[8,2]{0,1:T(2,128)S(1)} all-reduce(f32[8,2]{0,1:T(2,128)S(1)} %multiply_reduce_fusion.5), channel_id=1, replica_groups=mesh['site'=2,'wide'=32,'narrow'=4] {'wide'}, use_global_device_ids=true, to_apply=%region_2.3 | all-reduce | flops 16 | bytes 128 | tf_op jit(solution)/shard_map/psum | solution.py:36
  104.0 24.8 %all_to_all.201 = f32[32,8,256]{2,1,0:T(8,128)S(1)} all-to-all(f32[32,8,256]{2,1,0:T(8,128)S(1)} %stack.12), channel_id=1, replica_groups=mesh['site'=2,'wide'=32,'narrow'=4] {'wide'}, dimensions={0} | all-to-all | bytes 524288 | tf_op jit(solution)/shard_map/all_to_all | solution.py:42
  128.7 9.2 %all_to_all.202 = f32[8,4,2048]{2,0,1:T(8,128)S(1)} all-to-all(f32[8,4,2048]{2,0,1:T(8,128)S(1)} %bitcast.195), channel_id=1, replica_groups=mesh['site'=2,'wide'=32,'narrow'=4] {'narrow'}, dimensions={1} | all-to-all | bytes 524288 | tf_op jit(solution)/shard_map/all_to_all | solution.py:49
  137.9 5.3 fusion.5
  143.3 18.4 %reduce-scatter.9.cloned.1.call-done = f32[8,2,256]{2,0,1:T(8,128)} async-done(((f32[32,2,256]{2,0,1:T(8,128)}), f32[8,2,256]{2,0,1:T(8,128)}) %reduce-scatter.9.cloned.1.call-update) | async-done | bytes 16400 | tf_op jit(solution)/shard_map/reduce_scatter | solution.py:21
  162.6 63.2 %psum.43 = f32[8,2]{0,1:T(2,128)S(1)} all-reduce(f32[8,2]{0,1:T(2,128)S(1)} %multiply_reduce_fusion.4), channel_id=1, replica_groups=mesh['site'=2,'wide'=32,'narrow'=4] {'wide'}, use_global_device_ids=true, to_apply=%region_5.6 | all-reduce | flops 16 | bytes 128 | tf_op jit(solution)/shard_map/psum | solution.py:36
  226.7 25.5 %all_to_all.203 = f32[32,8,256]{2,1,0:T(8,128)} all-to-all(f32[32,8,256]{2,1,0:T(8,128)S(1)} %stack.13), channel_id=1, replica_groups=mesh['site'=2,'wide'=32,'narrow'=4] {'wide'}, dimensions={0} | all-to-all | bytes 524288 | tf_op jit(solution)/shard_map/all_to_all | solution.py:42
  252.2 3.4 all-to-all-start.3
  255.7 6.6 all-to-all-done.3
  262.4 1.5 collective-permute-done
  264.0 5.3 fusion.1
  269.4 18.4 %reduce-scatter.11.cloned.1.call-done = f32[8,2,256]{2,0,1:T(8,128)} async-done(((f32[32,2,256]{2,0,1:T(8,128)}), f32[8,2,256]{2,0,1:T(8,128)}) %reduce-scatter.11.cloned.1.call-update) | async-done | bytes 16400 | tf_op jit(solution)/shard_map/reduce_scatter | solution.py:21
  288.6 63.2 %psum.44 = f32[8,2]{0,1:T(2,128)S(1)} all-reduce(f32[8,2]{0,1:T(2,128)S(1)} %multiply_reduce_fusion.3), channel_id=1, replica_groups=mesh['site'=2,'wide'=32,'narrow'=4] {'wide'}, use_global_device_ids=true, to_apply=%region_8.9 | all-reduce | flops 16 | bytes 128 | tf_op jit(solution)/shard_map/psum | solution.py:36
  352.7 24.8 %all_to_all.204 = f32[32,8,256]{2,1,0:T(8,128)S(1)} all-to-all(f32[32,8,256]{2,1,0:T(8,128)S(1)} %stack.14), channel_id=1, replica_groups=mesh['site'=2,'wide'=32,'narrow'=4] {'wide'}, dimensions={0} | all-to-all | bytes 524288 | tf_op jit(solution)/shard_map/all_to_all | solution.py:42
  377.5 9.2 %all_to_all.205 = f32[8,4,2048]{2,0,1:T(8,128)S(1)} all-to-all(f32[8,4,2048]{2,0,1:T(8,128)S(1)} %bitcast.196), channel_id=1, replica_groups=mesh['site'=2,'wide'=32,'narrow'=4] {'narrow'}, dimensions={1} | all-to-all | bytes 524288 | tf_op jit(solution)/shard_map/all_to_all | solution.py:49
  386.7 5.3 fusion.4
  392.1 18.4 %reduce-scatter.13.cloned.1.call-done = f32[8,2,256]{2,0,1:T(8,128)} async-done(((f32[32,2,256]{2,0,1:T(8,128)}), f32[8,2,256]{2,0,1:T(8,128)}) %reduce-scatter.13.cloned.1.call-update) | async-done | bytes 16400 | tf_op jit(solution)/shard_map/reduce_scatter | solution.py:21
  411.3 63.2 %psum.45 = f32[8,2]{0,1:T(2,128)S(1)} all-reduce(f32[8,2]{0,1:T(2,128)S(1)} %multiply_reduce_fusion.2), channel_id=1, replica_groups=mesh['site'=2,'wide'=32,'narrow'=4] {'wide'}, use_global_device_ids=true, to_apply=%region_11.12 | all-reduce | flops 16 | bytes 128 | tf_op jit(solution)/shard_map/psum | solution.py:36
  475.5 24.8 %all_to_all.206 = f32[32,8,256]{2,1,0:T(8,128)S(1)} all-to-all(f32[32,8,256]{2,1,0:T(8,128)S(1)} %stack.15), channel_id=1, replica_groups=mesh['site'=2,'wide'=32,'narrow'=4] {'wide'}, dimensions={0} | all-to-all | bytes 524288 | tf_op jit(solution)/shard_map/all_to_all | solution.py:42
  500.2 9.2 %all_to_all.207 = f32[8,4,2048]{2,0,1:T(8,128)S(1)} all-to-all(f32[8,4,2048]{2,0,1:T(8,128)S(1)} %bitcast.197), channel_id=1, replica_groups=mesh['site'=2,'wide'=32,'narrow'=4] {'narrow'}, dimensions={1} | all-to-all | bytes 524288 | tf_op jit(solution)/shard_map/all_to_all | solution.py:49
  509.4 1.5 collective-permute-done.1
  511.0 5.3 fusion
  516.3 18.4 %reduce-scatter.15.cloned.1.call-done = f32[8,2,256]{2,0,1:T(8,128)} async-done(((f32[32,2,256]{2,0,1:T(8,128)}), f32[8,2,256]{2,0,1:T(8,128)}) %reduce-scatter.15.cloned.1.call-update) | async-done | bytes 16400 | tf_op jit(solution)/shard_map/reduce_scatter | solution.py:21
  535.5 63.2 %psum.46 = f32[8,2]{0,1:T(2,128)S(1)} all-reduce(f32[8,2]{0,1:T(2,128)S(1)} %multiply_reduce_fusion.1), channel_id=1, replica_groups=mesh['site'=2,'wide'=32,'narrow'=4] {'wide'}, use_global_device_ids=true, to_apply=%region_14.15 | all-reduce | flops 16 | bytes 128 | tf_op jit(solution)/shard_map/psum | solution.py:36
  599.7 25.5 %all_to_all.208 = f32[32,8,256]{2,1,0:T(8,128)} all-to-all(f32[32,8,256]{2,1,0:T(8,128)S(1)} %stack.16), channel_id=1, replica_groups=mesh['site'=2,'wide'=32,'narrow'=4] {'wide'}, dimensions={0} | all-to-all | bytes 524288 | tf_op jit(solution)/shard_map/all_to_all | solution.py:42
  625.1 3.4 all-to-all-start.9
  628.5 6.7 all-to-all-done.9
  635.8 3.2 all-to-all-start.12
  639.1 5.3 fusion.3
  644.9 4.8 all-to-all-start.13
  650.3 4.7 all-to-all-done.13
  655.7 3.2 all-to-all-start.14
  659.0 5.1 all-to-all-done.14
  664.7 3.2 all-to-all-start.15
  667.9 6.0 reduce-scatter.17.cloned.1.call-done
  674.8 63.2 %psum.47 = f32[8,2]{0,1:T(2,128)S(1)} all-reduce(f32[8,2]{0,1:T(2,128)S(1)} %multiply_reduce_fusion), channel_id=1, replica_groups=mesh['site'=2,'wide'=32,'narrow'=4] {'wide'}, use_global_device_ids=true, to_apply=%region_17.18 | all-reduce | flops 16 | bytes 128 | tf_op jit(solution)/shard_map/psum | solution.py:36
  738.6 3.2 all-to-all-start.16
  741.9 5.1 all-to-all-done.16
  747.6 3.2 all-to-all-start.17
  751.6 4.4 all-to-all-done.17
  756.7 16.6 %all-to-all-start.10 = ((f32[32,8,256]{2,1,0:T(8,128)}), f32[32,8,256]{2,1,0:T(8,128)}, u32[]{:S(2)}, u32[]{:S(2)}) async-start(f32[32,8,256]{2,1,0:T(8,128)} %stack.17), calls=%async_computation.16 | async-start | bytes 524288 | tf_op jit(solution)/shard_map/all_to_all | solution.py:42
  773.8 9.3 %all-to-all-done.10 = f32[32,8,256]{2,1,0:T(8,128)} async-done(((f32[32,8,256]{2,1,0:T(8,128)}), f32[32,8,256]{2,1,0:T(8,128)}, u32[]{:S(2)}, u32[]{:S(2)}) %all-to-all-start.10) | async-done | bytes 262176 | tf_op jit(solution)/shard_map/all_to_all | solution.py:42
  783.1 3.4 all-to-all-start.11
  787.0 6.1 all-to-all-done.11
  793.2 1.0 copy.12
  (72 shorter events, 17.0 us)
Async XLA Ops:
  7.2 255.1 %copy-start = (f32[32,1,2048]{2,1,0:T(1,128)S(1)}, f32[32,1,2048]{2,1,0:T(1,128)}, u32[]{:S(2)}) copy-start(f32[32,1,2048]{2,1,0:T(1,128)} %param.3) | copy-start | bytes 786436
  7.2 31.8 %reduce-scatter.7.cloned.1.call-start = ((), (), s32[]{:S(2)}) async-start(), calls=%async_computation.24 | async-start | bytes 81920 | tf_op jit(solution)/shard_map/reduce_scatter | solution.py:21
  12.7 149.0 %reduce-scatter.9.cloned.1.call-start = ((), (), s32[]{:S(2)}) async-start(), calls=%async_computation.25 | async-start | bytes 81920 | tf_op jit(solution)/shard_map/reduce_scatter | solution.py:21
  252.2 10.1 %all-to-all-start.3 = ((f32[8,4,2048]{2,0,1:T(8,128)}), f32[8,4,2048]{2,0,1:T(8,128)S(1)}, u32[]{:S(2)}, u32[]{:S(2)}) async-start(f32[8,4,2048]{2,0,1:T(8,128)} %bitcast.21), calls=%async_computation.5 | async-start | bytes 524288 | tf_op jit(solution)/shard_map/all_to_all | solution.py:49
  255.6 32.1 %reduce-scatter.11.cloned.1.call-start = ((), (), s32[]{:S(2)}) async-start(), calls=%async_computation.26 | async-start | bytes 81920 | tf_op jit(solution)/shard_map/reduce_scatter | solution.py:21
  262.3 1.6 collective-permute-start
  269.3 141.2 %reduce-scatter.13.cloned.1.call-start = ((), (), s32[]{:S(2)}) async-start(), calls=%async_computation.27 | async-start | bytes 81920 | tf_op jit(solution)/shard_map/reduce_scatter | solution.py:21
  392.0 142.7 %reduce-scatter.15.cloned.1.call-start = ((), (), s32[]{:S(2)}) async-start(), calls=%async_computation.28 | async-start | bytes 81920 | tf_op jit(solution)/shard_map/reduce_scatter | solution.py:21
  509.4 1.5 collective-permute-start.1
  625.1 10.1 %all-to-all-start.9 = ((f32[8,4,2048]{2,0,1:T(8,128)}), f32[8,4,2048]{2,0,1:T(8,128)S(1)}, u32[]{:S(2)}, u32[]{:S(2)}) async-start(f32[8,4,2048]{2,0,1:T(8,128)} %bitcast.50), calls=%async_computation.14 | async-start | bytes 524288 | tf_op jit(solution)/shard_map/all_to_all | solution.py:49
  635.8 8.6 %all-to-all-start.12 = ((f32[8,4,1]{0,2,1:T(1,128)}), f32[8,4,1]{0,2,1:T(1,128)S(1)}, u32[]{:S(2)}, u32[]{:S(2)}) async-start(f32[8,4,1]{0,2,1:T(1,128)} %broadcast_in_dim.96), calls=%async_computation.18 | async-start | bytes 4096 | tf_op jit(solution)/shard_map/all_to_all | solution.py:50
  644.9 10.0 %all-to-all-start.13 = ((f32[8,4,1]{0,2,1:T(1,128)}), f32[8,4,1]{0,2,1:T(1,128)S(1)}, u32[]{:S(2)}, u32[]{:S(2)}) async-start(f32[8,4,1]{0,2,1:T(1,128)} %broadcast_in_dim.97), calls=%async_computation.19 | async-start | bytes 4096 | tf_op jit(solution)/shard_map/all_to_all | solution.py:50
  649.7 24.2 %reduce-scatter.17.cloned.1.call-start = ((), (), s32[]{:S(2)}) async-start(), calls=%async_computation.29 | async-start | bytes 81920 | tf_op jit(solution)/shard_map/reduce_scatter | solution.py:21
  655.7 8.4 %all-to-all-start.14 = ((f32[8,4,1]{0,2,1:T(1,128)}), f32[8,4,1]{0,2,1:T(1,128)S(1)}, u32[]{:S(2)}, u32[]{:S(2)}) async-start(f32[8,4,1]{0,2,1:T(1,128)} %broadcast_in_dim.99), calls=%async_computation.20 | async-start | bytes 4096 | tf_op jit(solution)/shard_map/all_to_all | solution.py:50
  658.9 114.6 %collective-permute-start.2 = (f32[32]{0:T(128)S(1)}, f32[32]{0:T(128)S(1)}, u32[]{:S(2)}, u32[]{:S(2)}) collective-permute-start(f32[32]{0:T(128)S(1)} %select_n.137), channel_id=1, source_target_pairs={{0,128},{128,0},{1,129},{129,1},{2,130},{130,2},{3,131},{131,3},{4... | collective-permute-start | bytes 392 | tf_op jit(solution)/shard_map/ppermute | solution.py:14
  664.7 73.3 %all-to-all-start.15 = ((f32[8,4,1]{0,2,1:T(1,128)}), f32[8,4,1]{0,2,1:T(1,128)S(1)}, u32[]{:S(2)}, u32[]{:S(2)}) async-start(f32[8,4,1]{0,2,1:T(1,128)} %broadcast_in_dim.100), calls=%async_computation.21 | async-start | bytes 4096 | tf_op jit(solution)/shard_map/all_to_all | solution.py:50
  738.6 8.4 %all-to-all-start.16 = ((f32[8,4,1]{0,2,1:T(1,128)}), f32[8,4,1]{0,2,1:T(1,128)S(1)}, u32[]{:S(2)}, u32[]{:S(2)}) async-start(f32[8,4,1]{0,2,1:T(1,128)} %broadcast_in_dim.101), calls=%async_computation.22 | async-start | bytes 4096 | tf_op jit(solution)/shard_map/all_to_all | solution.py:50
  747.6 8.4 %all-to-all-start.17 = ((f32[8,4,1]{0,2,1:T(1,128)}), f32[8,4,1]{0,2,1:T(1,128)S(1)}, u32[]{:S(2)}, u32[]{:S(2)}) async-start(f32[8,4,1]{0,2,1:T(1,128)} %broadcast_in_dim.102), calls=%async_computation.23 | async-start | bytes 4096 | tf_op jit(solution)/shard_map/all_to_all | solution.py:50
  756.7 26.3 %all-to-all-start.10 = ((f32[32,8,256]{2,1,0:T(8,128)}), f32[32,8,256]{2,1,0:T(8,128)}, u32[]{:S(2)}, u32[]{:S(2)}) async-start(f32[32,8,256]{2,1,0:T(8,128)} %stack.17), calls=%async_computation.16 | async-start | bytes 524288 | tf_op jit(solution)/shard_map/all_to_all | solution.py:42
  773.4 13.0 %collective-permute-start.3 = (f32[32]{0:T(128)S(1)}, f32[32]{0:T(128)S(1)}, u32[]{:S(2)}, u32[]{:S(2)}) collective-permute-start(f32[32]{0:T(128)S(1)} %add_add_fusion), channel_id=1, source_target_pairs={{0,128},{128,0},{1,129},{129,1},{2,130},{130,2},{3,131},{131,3},{4... | collective-permute-start | bytes 392 | tf_op jit(solution)/shard_map/ppermute | solution.py:14
  783.1 10.1 %all-to-all-start.11 = ((f32[8,4,2048]{2,0,1:T(8,128)}), f32[8,4,2048]{2,0,1:T(8,128)S(1)}, u32[]{:S(2)}, u32[]{:S(2)}) async-start(f32[8,4,2048]{2,0,1:T(8,128)} %bitcast.59), calls=%async_computation.17 | async-start | bytes 524288 | tf_op jit(solution)/shard_map/all_to_all | solution.py:49
Sparse Core Ops, SparseCore 0:
  12.8 26.1 reduce-scatter.6
  143.4 18.2 reduce-scatter.8
  269.4 18.2 reduce-scatter.10
  392.1 18.2 reduce-scatter.12
  516.4 18.2 reduce-scatter.14
  653.2 20.6 reduce-scatter.16
